TPU v7x, 512 devices: a whole 4x8x8 slice. The times are simulated.
512 devices in a mesh: tok: 32 (over y, x), layer: 16 (over z, core).
Axes of the slice: x: 4, y: 8, z: 8, core: 2. Of those that a mesh axis runs over, the one named last changes fastest.
Arguments:
- activations: bfloat16 [16, 14336, 5120], P(None, ('tok', 'layer')), may hold values from -9 to 9
- pos_weight: bfloat16 [16, 48, 5120], P('layer', None, 'tok'), may hold values from -1 to 1
- depth_weight: bfloat16 [16, 128, 5120], P('layer', None, 'tok'), may hold values from -0.01953125 to 0.01953125
- tags: int32 [14336], P(('tok', 'layer')), may hold values from 0 to 47
- depths: int32 [14336], P(('tok', 'layer')), may hold values from 2 to 14
- counts: int32 [512], P(('tok', 'layer')), may hold values from 1 to 28, 8960 in all
Outputs:
- pos_grad: float32 [16, 48, 5120], P('layer', None, 'tok')
- depth_grad: float32 [16, 128, 5120], P('layer', None, 'tok')
Inputs may be any that keep to these rules, and one draw needn't show every extreme that they name: counts[d] is the number of live slots among device d's 28 slots, which are its first ones; the largest count equals 28.
All inputs are finite; a program needn't handle non-finite values.
Results may differ from a plain program's by a relative error of at most 0.0042.
Values may be sent and summed in bfloat16 or wider, within the bound.
A program may use at most 64 MiB of HBM per device.

v0:
```python
import jax
import jax.numpy as jnp
from jax import lax
from jax.sharding import PartitionSpec as P


def gather_turned(arrays, axis, dims):
    turned = [jnp.moveaxis(a, dim, 0) for a, dim in zip(arrays, dims)]
    widths = [t[0].size for t in turned]
    both = jnp.concatenate([t.reshape(-1, w) for t, w in zip(turned, widths)], axis=1)
    filled = lax.all_gather(both, axis, axis=0, tiled=True)
    blocks = jnp.split(filled, [sum(widths[:k]) for k in range(1, len(widths))], axis=1)
    return tuple(
        (
            jnp.moveaxis(b.reshape(-1, *t.shape[1:]), 0, dim)
            for b, t, dim in zip(blocks, turned, dims)
        )
    )


def in_blocks(shard, dim, devices):
    before, after = (shard.shape[:dim], shard.shape[dim + 1 :])
    return jnp.moveaxis(shard.reshape(*before, devices, -1, *after), dim, 0)


def sum_at_owner(shard, axis, dim):
    blocks = in_blocks(shard, dim, lax.axis_size(axis))
    arrived = lax.all_to_all(blocks, axis, split_axis=0, concat_axis=0, tiled=True)
    return arrived.astype(jnp.float32).sum(axis=0)


def contract(left, right):
    return lax.dot_general(
        left, right, (((1,), (1,)), ((), ())), preferred_element_type=jnp.float32
    )


def local(activations, pos_weight, depth_weight, tags, depths, counts):
    tag_count = pos_weight.shape[1]
    rank_count = depth_weight.shape[1]
    slots_each = tags.shape[0]
    pos_full, depth_full = gather_turned((pos_weight, depth_weight), "tok", (2, 2))
    stacked = activations.reshape(
        (activations.shape[0], 1, activations.shape[1], activations.shape[2])
    )
    arrived = lax.all_to_all(stacked, "layer", split_axis=0, concat_axis=1, tiled=True)
    flat = arrived.reshape((-1, arrived.shape[3]))
    shape = arrived.shape[:3]
    first = contract(flat, pos_full[0]).reshape(shape + (tag_count,))
    second = contract(flat, depth_full[0]).reshape(shape + (rank_count,))
    arrived, first, second = (arrived, first, second)
    owned_rows = arrived.reshape((-1, arrived.shape[3]))
    logits = first.reshape((-1, tag_count))
    hidden = second.reshape((-1, rank_count))
    tag_rows, depth_rows, block_counts = (
        lax.all_gather(tags, "layer", axis=0, tiled=True),
        lax.all_gather(depths, "layer", axis=0, tiled=True),
        lax.all_gather(counts, "layer", axis=0, tiled=True),
    )
    row_count = owned_rows.shape[0]
    slot_index = jnp.arange(row_count, dtype=jnp.int32)
    position = slot_index % slots_each
    block_index = slot_index // slots_each
    source_index = jnp.arange(block_counts.shape[0], dtype=jnp.int32)
    match = block_index[:, None] == source_index[None, :]
    block_count = jnp.sum(jnp.where(match, block_counts[None, :], 0), axis=1)
    live = position < block_count
    token_scale = jnp.where(live, 1.0 / block_count.astype(jnp.float32), jnp.float32(0.0))
    top = jnp.max(logits, axis=1, keepdims=True)
    expo = jnp.exp(logits - top)
    probabilities = expo / jnp.sum(expo, axis=1, keepdims=True)
    onehot = (tag_rows[:, None] == jnp.arange(tag_count, dtype=jnp.int32)[None, :]).astype(
        jnp.float32
    )
    g_pos = (probabilities - onehot) * token_scale[:, None]
    predicted = jnp.sum(hidden * hidden, axis=1)
    residual = predicted - depth_rows.astype(jnp.float32)
    g_depth = hidden * (residual * token_scale)[:, None]
    joined = jnp.concatenate([g_pos, g_depth], axis=1).astype(jnp.bfloat16)
    summed = sum_at_owner(
        lax.dot_general(
            owned_rows, joined, (((0,), (0,)), ((), ())), preferred_element_type=jnp.float32
        ).astype(jnp.bfloat16),
        "tok",
        0,
    ).T
    return (summed[None, :tag_count], summed[None, tag_count:])


def solution(mesh):
    in_specs = (
        P(None, ("tok", "layer"), None),
        P("layer", None, "tok"),
        P("layer", None, "tok"),
        P(("tok", "layer")),
        P(("tok", "layer")),
        P(("tok", "layer")),
    )
    out_specs = (P("layer", None, "tok"), P("layer", None, "tok"))
    return jax.shard_map(local, mesh=mesh, in_specs=in_specs, out_specs=out_specs, check_vma=False)
```

profile of v0, /device:TPU:1, one launch (start us, length us, event | category | flops | bytes accessed | tf_op | source)
XLA Modules:
  0.0 249.2 jit_solution(1745421143395113516)
XLA Ops:
  7.2 7.2 %copy.31 = bf16[16,28,5120]{2,1,0:T(8,128)(2,1)} copy(bf16[16,28,5120]{2,0,1:T(8,128)(2,1)} %param.6) | data formatting | bytes 9175040 | tf_op args[0]
  14.4 0.0 copy-start.2
  14.4 0.0 copy-start.1
  14.4 0.0 copy-start.4
  14.4 12.0 %all-to-all-start = ((bf16[16,1,28,5120]{3,2,1,0:T(8,128)(2,1)}), bf16[16,1,28,5120]{3,2,1,0:T(8,128)(2,1)}, u32[]{:S(2)}, u32[]{:S(2)}) async-start(bf16[16,1,28,5120]{3,2,1,0:T(8,128)(2,1)} %bitcast.47), calls=%async_computation | async-start | bytes 10485760 | tf_op jit(solution)/shard_map/all_to_all | solution.py:46
  26.3 0.0 all-gather.2.cloned.1.call-start
  26.4 0.0 copy-done.2
  26.4 0.1 copy.24
  26.5 0.0 copy-done.1
  26.5 0.7 pad_maximum_fusion
  27.3 0.0 all-gather.2.cloned.1.call-update
  27.9 1.3 dynamic-slice
  29.9 0.0 copy-done.3
  29.9 0.2 dynamic-update-slice.2
  30.1 0.0 copy-done.4
  30.1 0.2 dynamic-update-slice
  30.3 0.8 dynamic-update-slice.1
  31.1 117.2 %all-reduce.3 = (s32[16]{0:T(128)S(1)}, s32[448]{0:T(512)S(1)}, s32[448]{0:T(512)S(1)}) all-reduce(s32[16]{0:T(128)S(1)} %dynamic-update-slice.1, s32[448]{0:T(512)S(1)} %dynamic-update-slice.2, s32[448]{0:T(512)S(1)} %dynamic-update-slice), channel_id=1, replica_groups=mesh['tok'=32,'layer'=16] {'layer'}, use_global_device_ids=true, to_apply=%add.1 | all-reduce | flops 912 | bytes 7296
  148.3 0.1 select_reduce_fusion
  148.4 0.0 all-to-all-done
  148.4 7.2 %reshape.65 = bf16[448,5120]{1,0:T(8,128)(2,1)} reshape(bf16[16,1,28,5120]{3,2,1,0:T(8,128)(2,1)} %all-to-all-done) | data formatting | bytes 9175040 | tf_op jit(solution)/shard_map/reshape | solution.py:52
  155.6 4.3 %fusion.17 = (f32[448]{0:T(512)S(1)}, f32[48,448]{1,0:T(8,128)S(1)}) fusion(bf16[448,5120]{1,0:T(8,128)(2,1)} %reshape.65, bf16[5120,176]{1,0:T(8,128)(2,1)} %all-gather.2.cloned.1.call-done), kind=kOutput, calls=%fused_computation.38 | convolution fusion | flops 220222016 | bytes 5986048 | tf_op jit(solution)/shard_map/dot_general | solution.py:33
  159.9 0.0 copy-done
  160.0 3.3 %multiply_reduce_fusion = (f32[448]{0:T(512)S(1)}, f32[128,448]{0,1:T(8,128)S(1)}) fusion(bf16[448,5120]{1,0:T(8,128)(2,1)S(1)} %copy-done, bf16[5120,176]{1,0:T(8,128)(2,1)} %all-gather.2.cloned.1.call-done), kind=kOutput, calls=%fused_computation.12 | convolution fusion | flops 587316800 | bytes 6129408 | tf_op jit(solution)/shard_map/dot_general | solution.py:33
  163.3 0.1 copy.26
  163.4 0.1 fusion.6
  163.6 4.8 %fusion = bf16[5120,176]{0,1:T(8,128)(2,1)} fusion(bf16[448,5120]{1,0:T(8,128)(2,1)} %reshape.65, bf16[448,128]{1,0:T(8,128)(2,1)S(1)} %fusion.6, bf16[448,48]{1,0:T(8,128)(2,1)S(1)} %copy.26), kind=kOutput, calls=%fused_computation.1 | convolution fusion | flops 808620032 | bytes 6547456 | tf_op jit(solution)/shard_map/dot_general | solution.py:81
  168.3 3.0 %copy.29 = bf16[5120,176]{1,0:T(8,128)(2,1)S(1)} copy(bf16[5120,176]{0,1:T(8,128)(2,1)} %fusion) | data formatting | bytes 3604480 | tf_op jit(solution)/shard_map/reshape | solution.py:23
  171.4 69.1 %all_to_all.14 = bf16[32,160,176]{2,1,0:T(8,128)(2,1)S(1)} all-to-all(bf16[32,160,176]{2,1,0:T(8,128)(2,1)S(1)} %bitcast.48), channel_id=1, replica_groups=mesh['tok'=32,'layer'=16] {'tok'}, dimensions={0} | all-to-all | bytes 3604480 | tf_op jit(solution)/shard_map/all_to_all | solution.py:28
  240.5 0.4 convert_reduce_fusion
  240.9 0.7 slice_bitcast_fusion.4
  241.6 0.7 copy.28
  (11 shorter events, 0.1 us)
Async XLA Ops:
  14.4 12.0 %copy-start.2 = (bf16[1,48,160]{2,1,0:T(8,128)(2,1)S(1)}, bf16[1,48,160]{2,1,0:T(8,128)(2,1)}, u32[]{:S(2)}) copy-start(bf16[1,48,160]{2,1,0:T(8,128)(2,1)} %param.7) | copy-start | bytes 46084
  14.4 12.1 %copy-start.1 = (bf16[1,128,160]{1,2,0:T(8,128)(2,1)S(1)}, bf16[1,128,160]{1,2,0:T(8,128)(2,1)}, u32[]{:S(2)}) copy-start(bf16[1,128,160]{1,2,0:T(8,128)(2,1)} %param.8) | copy-start | bytes 122884
  14.4 15.5 %copy-start.3 = (s32[28]{0:T(128)S(1)}, s32[28]{0:T(128)}, u32[]{:S(2)}) copy-start(s32[28]{0:T(128)} %param.10) | copy-start | bytes 340
  14.4 15.7 %copy-start.4 = (s32[28]{0:T(128)S(1)}, s32[28]{0:T(128)}, u32[]{:S(2)}) copy-start(s32[28]{0:T(128)} %param.9) | copy-start | bytes 340
  14.4 134.0 %all-to-all-start = ((bf16[16,1,28,5120]{3,2,1,0:T(8,128)(2,1)}), bf16[16,1,28,5120]{3,2,1,0:T(8,128)(2,1)}, u32[]{:S(2)}, u32[]{:S(2)}) async-start(bf16[16,1,28,5120]{3,2,1,0:T(8,128)(2,1)} %bitcast.47), calls=%async_computation | async-start | bytes 10485760 | tf_op jit(solution)/shard_map/all_to_all | solution.py:46
  26.3 129.3 %all-gather.2.cloned.1.call-start = ((), (), s32[]{:S(2)}) async-start(), calls=%async_computation.2 | async-start | bytes 2703360 | tf_op jit(solution)/shard_map/all_gather | solution.py:11
  155.6 4.3 %copy-start = (bf16[448,5120]{1,0:T(8,128)(2,1)S(1)}, bf16[448,5120]{1,0:T(8,128)(2,1)}, u32[]{:S(2)}) copy-start(bf16[448,5120]{1,0:T(8,128)(2,1)} %reshape.65) | copy-start | bytes 13762564
Sparse Core Ops, SparseCore 0:
  30.9 80.8 all-gather.1
where the time goes:
time: 252 us; the launch traced here: 249 us
  blocking collectives  186 us (74%)
  local copies, waits for them, and re-layouts  21.7 us (9%)
  between operations  15.4 us (6%)
  matrix products  12.3 us (5%)
  starting transfers between devices  12 us (5%)
    unnamed x1, blocking collectives  117 us
    all_to_all x1, blocking collectives, sum_at_owner(): lax.all_to_all(blocks, axis, split_axis=0, concat_axis=0, tiled=True)  69.1 us
    all_to_all x1, starting transfers between devices, local(): lax.all_to_all(stacked, 'layer', split_axis=0, concat_axis=1, tiled=True)  12 us
    unnamed x19, local copies, waits for them, and re-layouts  9.84 us
    dot_general x2, matrix products, contract(): lax.dot_general(left, right, (((1,), (1,)), ((), ())), preferred_element_...  7.53 us
    reshape x1, local copies, waits for them, and re-layouts, local(): owned_rows = arrived.reshape((-1, arrived.shape[3]))  7.25 us
  transfers between devices with their start and end apart: 2, of which 0 were waited for; matrix products, arithmetic and copies ran while one was open for 4% of the time, Pallas kernels for 0%

commit v1 on v0

v1 whole, which is shorter than its diff:
```python
import jax
import jax.numpy as jnp
from jax import lax
from jax.experimental import pallas as pl
from jax.experimental.pallas import tpu as pltpu
from jax.sharding import PartitionSpec as P

MESH = pl.DeviceIdType.MESH
F32, BF16 = jnp.float32, jnp.bfloat16

D, TAGS, RANK, SLOTS = 5120, 48, 128, 28
K = TAGS + RANK
PAD = 32
NX, NY, NQ, NR = 4, 8, 4, 4
GROUP = NX * NR
CHUNKS, WIDE = 4, D // 4
OWN = D // NY
SUBS = ((0, 96), (96, 80))
PARTS = ((0, 24), (24, 4))
PARTNERS = tuple((dx, dr) for dr in range(NR) for dx in (1, 3, 2, 0) if (dx, dr) != (0, 0))


def place():
    tok, lay = lax.axis_index("tok"), lax.axis_index("layer")
    return lax.div(tok, NX), lax.rem(tok, NX), lax.div(lay, NR), lax.rem(lay, NR)


def dev(y, x, q, r):
    return {"tok": y * NX + x, "layer": q * NR + r}


def wrap(v, n):
    return lax.rem(v + n, n)


def send(src, dst, ssem, rsem, device):
    return pltpu.make_async_remote_copy(
        src_ref=src, dst_ref=dst, send_sem=ssem, recv_sem=rsem, device_id=device, device_id_type=MESH
    )


def kernel(
    x_hbm, w_ref, meta_ref, pos_out, dep_out,
    xin, outbox, rows, wwin, wx, wf, meta_own, meta_in, acc, g_ref,
    right_out, right_in, left_out, left_in, mine, r2_in, r3_in,
    load_sem, act_s, act_r, w_s, w_r, wr_s, wr_r, wl_s, wl_r, meta_s, meta_r,
    rr_s, rr_r, rl_s, rl_r, r2_s, r2_r, r3_s, r3_r,
):
    y, x, q, r = place()
    me = x * NR + r
    here = dev(y, x, q, r)
    up, down = dev(wrap(y + 1, NY), x, q, r), dev(wrap(y - 1, NY), x, q, r)

    def partner(dx, dr):
        px, pr = wrap(x + dx, NX), wrap(r + dr, NR)
        return px * NR + pr, dev(y, px, q, pr)

    loads = [
        pltpu.make_async_copy(x_hbm.at[:, pl.ds(k * WIDE, WIDE)], xin.at[k], load_sem.at[k])
        for k in range(CHUNKS)
    ]
    for c in loads:
        c.start()
    rows[:, 16:PAD, :] = jnp.zeros((GROUP, PAD - 16, D), BF16)
    home = x == q

    barrier = pltpu.get_barrier_semaphore()

    def greet(device):
        pl.semaphore_signal(barrier, inc=1, device_id=device, device_id_type=MESH)

    for dx, dr in PARTNERS:
        greet(partner(dx, dr)[1])
    for d in range(1, NQ):
        greet(dev(y, x, wrap(q + d, NQ), r))
    greet(up)
    greet(down)
    for sx in range(NX):
        @pl.when(jnp.logical_or(sx != x, q != x))
        def _():
            greet(dev(y, sx, x, r))

    wwin[...] = pltpu.roll(w_ref[...].astype(F32), 32 * x, 1).astype(BF16)
    meta_own[...] = pltpu.roll(meta_ref[...], 32 * r, 1)
    pl.semaphore_wait(barrier, len(PARTNERS) + NQ - 1 + 2 + NX - home.astype(jnp.int32))

    def w_send(q2):
        return send(wwin, wx.at[x], w_s.at[q2], w_r.at[x], dev(y, q, q2, r))

    for q2 in range(NQ):
        @pl.when(jnp.logical_not(jnp.logical_and(home, q2 == q)))
        def _():
            w_send(q2).start()

    @pl.when(home)
    def _():
        wx[x] = wwin[...]

    def meta_send(i, dx, dr):
        slot, device = partner(dx, dr)
        return send(meta_own, meta_in.at[me], meta_s.at[i], meta_r.at[me], device)

    for i, (dx, dr) in enumerate(PARTNERS):
        meta_send(i, dx, dr).start()
    meta_in[me] = meta_own[...]

    ri = lax.broadcasted_iota(jnp.int32, (256, 256), 0)
    ci = lax.broadcasted_iota(jnp.int32, (256, 256), 1)
    turn = jnp.where(ci == lax.rem(ri, 16) * 16 + lax.div(ri, 16), 1.0, 0.0).astype(BF16)

    def act_send(k, i, j):
        dx, dr = PARTNERS[i]
        slot, device = partner(dx, dr)
        lo, n = PARTS[j]
        return send(
            outbox.at[k, slot, pl.ds(lo, n)],
            rows.at[me, pl.ds(lo, n), pl.ds(k * WIDE, WIDE)],
            act_s.at[k, i, j], act_r.at[k, me, j], device,
        )

    def turn_and_send(k):
        loads[k].wait()

        @pl.loop(0, WIDE // 256)
        def _(b):
            cols = pl.ds(pl.multiple_of(b * 256, 256), 256)
            first = jnp.dot(turn, xin[k, 0:256, cols], preferred_element_type=F32)
            outbox[k, :, 0:16, cols] = first.astype(BF16).reshape(16, 16, 256)
            last = jnp.dot(turn[:, 0:192], xin[k, 256:448, cols], preferred_element_type=F32)
            outbox[k, :, 16:32, cols] = last.astype(BF16).reshape(16, 16, 256)

        for i in range(len(PARTNERS)):
            for j in range(2):
                act_send(k, i, j).start()
        rows[me, :, k * WIDE:(k + 1) * WIDE] = outbox[k, me]

    for k in range(CHUNKS):
        turn_and_send(k)

    for sx in range(NX):
        @pl.when(jnp.logical_or(sx != x, q != x))
        def _():
            send(wwin, wx.at[sx], w_s.at[0], w_r.at[sx], dev(y, sx, x, r)).wait_recv()
    for t in range(5):
        part = None
        for sx in (t - 1, t):
            if 0 <= sx < NX:
                lo = 128 * (t - sx)
                v = wx[sx, :, lo:lo + 128].astype(F32)
                part = v if part is None else part + v
        wf[y, :, 128 * t:128 * (t + 1)] = part.astype(BF16)

    def ring(s, way):
        at = wrap(y - s, NY) if way > 0 else wrap(y + s, NY)
        ss, rs = (wr_s, wr_r) if way > 0 else (wl_s, wl_r)
        return send(wf.at[at], wf.at[at], ss.at[s], rs.at[s], up if way > 0 else down)

    for s in range(4):
        for way, steps in ((1, 4), (-1, 3)):
            if s < steps:
                if s > 0:
                    ring(s - 1, way).wait_recv()
                ring(s, way).start()
    ring(3, 1).wait_recv()
    ring(2, -1).wait_recv()

    acc[...] = jnp.zeros_like(acc)

    @pl.loop(0, CHUNKS)
    def _(k):
        for i, (dx, dr) in enumerate(PARTNERS):
            slot, device = partner(dx, dr)
            for j, (lo, n) in enumerate(PARTS):
                send(
                    outbox.at[0, slot, pl.ds(lo, n)],
                    rows.at[slot, pl.ds(lo, n), pl.ds(pl.multiple_of(k * WIDE, WIDE), WIDE)],
                    act_s.at[k, i, j], act_r.at[k, slot, j], device,
                ).wait_recv()
        for h in range(2):
            cols = pl.ds(pl.multiple_of(k * WIDE + h * OWN, 128), OWN)
            acc[...] += lax.dot_general(
                wf[2 * k + h], rows[:, :, cols].reshape(GROUP * PAD, OWN),
                (((1,), (1,)), ((), ())), preferred_element_type=F32,
            )

    for i, (dx, dr) in enumerate(PARTNERS):
        slot, device = partner(dx, dr)
        send(meta_own, meta_in.at[slot], meta_s.at[i], meta_r.at[slot], device).wait_recv()
    facts = jnp.concatenate(
        [sum(meta_in[NR * sx + sr] for sr in range(NR)) for sx in range(NX)], axis=1
    )
    tags, depths, scale = facts[0:1], facts[1:2], facts[2:3]
    logits, hidden = acc[0:TAGS], acc[TAGS:K]
    expo = jnp.exp(logits - jnp.max(logits, axis=0, keepdims=True))
    probs = expo / jnp.sum(expo, axis=0, keepdims=True)
    names = lax.broadcasted_iota(jnp.int32, (TAGS, GROUP * PAD), 0).astype(F32)
    onehot = jnp.where(names == tags, 1.0, 0.0)
    g_ref[0:TAGS] = ((probs - onehot) * scale).astype(BF16)
    predicted = jnp.sum(hidden * hidden, axis=0, keepdims=True)
    g_ref[TAGS:K] = (hidden * ((predicted - depths) * scale)).astype(BF16)

    def block(at, sub):
        lo, n = sub
        cols = pl.ds(pl.multiple_of(at * OWN, 128), OWN)
        return jnp.dot(
            g_ref[lo:lo + n], rows[:, :, cols].reshape(GROUP * PAD, OWN), preferred_element_type=F32
        )

    def hop(s, u, way):
        lo, n = SUBS[u]
        out, inn, ss, rs = (right_out, right_in, rr_s, rr_r) if way > 0 else (left_out, left_in, rl_s, rl_r)
        return send(
            out.at[s, pl.ds(lo, n)], inn.at[s, pl.ds(lo, n)], ss.at[s, u], rs.at[s, u],
            up if way > 0 else down,
        )

    for s in range(4):
        for u, (lo, n) in enumerate(SUBS):
            for way, steps in ((1, 4), (-1, 3)):
                if s >= steps:
                    continue
                out, inn = (right_out, right_in) if way > 0 else (left_out, left_in)
                at = wrap(y + 4 - s, NY) if way > 0 else wrap(y - 3 + s, NY)
                value = block(at, (lo, n))
                if s > 0:
                    hop(s - 1, u, way).wait_recv()
                    value = value + inn[s - 1, lo:lo + n].astype(F32)
                out[s, lo:lo + n] = value.astype(BF16)
                hop(s, u, way).start()
    for u, (lo, n) in enumerate(SUBS):
        value = block(y, (lo, n))
        hop(2, u, -1).wait_recv()
        value = value + left_in[2, lo:lo + n].astype(F32)
        hop(3, u, 1).wait_recv()
        mine[lo:lo + n] = (value + right_in[3, lo:lo + n].astype(F32)).astype(BF16)

    def r2(dx):
        px = wrap(x + dx, NX)
        return send(
            mine.at[:, pl.ds(pl.multiple_of(128 * px, 128), 256)], r2_in.at[x],
            r2_s.at[dx], r2_r.at[x], dev(y, px, q, r),
        )

    for dx in (1, 3, 2):
        r2(dx).start()
    r2_in[x] = mine[:, pl.ds(pl.multiple_of(128 * x, 128), 256)]

    def r3(dq):
        pq = wrap(q + dq, NQ)
        return send(r2_in.at[pq], r3_in.at[q], r3_s.at[dq], r3_r.at[q], dev(y, x, pq, r))

    def r2_arrived(sx):
        @pl.when(sx != x)
        def _():
            send(mine.at[:, pl.ds(0, 256)], r2_in.at[sx], r2_s.at[0], r2_r.at[sx], dev(y, sx, q, r)).wait_recv()

    for dq in (1, 3, 2):
        r2_arrived(wrap(q + dq, NQ))
        r3(dq).start()
    r2_arrived(q)
    total = r2_in[q].astype(F32)
    for dq in (1, 3, 2):
        sq = wrap(q + dq, NQ)
        send(mine.at[:, pl.ds(0, 256)], r3_in.at[sq], r3_s.at[0], r3_r.at[sq], dev(y, x, sq, r)).wait_recv()
        total = total + r3_in[sq].astype(F32)
    total = pltpu.roll(total, lax.rem(256 - 32 * x, 256), 1)
    pos_out[...] = total[0:TAGS, 0:160]
    dep_out[...] = total[TAGS:K].T[0:160]

    for q2 in range(NQ):
        @pl.when(jnp.logical_not(jnp.logical_and(home, q2 == q)))
        def _():
            w_send(q2).wait_send()
    for i, (dx, dr) in enumerate(PARTNERS):
        meta_send(i, dx, dr).wait_send()
        for k in range(CHUNKS):
            for j in range(2):
                act_send(k, i, j).wait_send()
    for s in range(4):
        for way, steps in ((1, 4), (-1, 3)):
            if s < steps:
                ring(s, way).wait_send()
                for u in range(2):
                    hop(s, u, way).wait_send()
    for d in (1, 3, 2):
        r2(d).wait_send()
        r3(d).wait_send()


def local(activations, pos_weight, depth_weight, tags, depths, counts):
    acts = jnp.transpose(activations, (1, 0, 2)).reshape(SLOTS * 16, D)
    probes = jnp.pad(jnp.concatenate([pos_weight[0], depth_weight[0]], axis=0), ((0, 0), (0, 96)))
    lane = jnp.arange(128, dtype=jnp.int32)
    count = counts[0]
    scale = jnp.where(lane < count, 1.0 / count.astype(F32), F32(0.0))
    wide = lambda v: jnp.pad(v.astype(F32), (0, 128 - SLOTS))
    facts = jnp.pad(jnp.stack([wide(tags), wide(depths), scale]), ((0, 5), (0, 0)))
    dma, vm = pltpu.SemaphoreType.DMA, pltpu.VMEM
    pos, dep = pl.pallas_call(
        kernel,
        out_shape=(jax.ShapeDtypeStruct((TAGS, 160), F32), jax.ShapeDtypeStruct((160, RANK), F32)),
        in_specs=[pl.BlockSpec(memory_space=pl.ANY), pl.BlockSpec(memory_space=vm), pl.BlockSpec(memory_space=vm)],
        out_specs=(pl.BlockSpec(memory_space=vm), pl.BlockSpec(memory_space=vm)),
        scratch_shapes=[
            vm((CHUNKS, SLOTS * 16, WIDE), BF16), vm((CHUNKS, 16, PAD, WIDE), BF16), vm((GROUP, PAD, D), BF16),
            vm((K, 256), BF16), vm((NX, K, 256), BF16), vm((NY, K, OWN), BF16),
            vm((8, 128), F32), vm((GROUP, 8, 128), F32), vm((K, GROUP * PAD), F32), vm((K, GROUP * PAD), BF16),
            vm((4, K, OWN), BF16), vm((4, K, OWN), BF16), vm((3, K, OWN), BF16), vm((3, K, OWN), BF16),
            vm((K, OWN), BF16), vm((NX, K, 256), BF16), vm((NQ, K, 256), BF16),
            dma((CHUNKS,)), dma((CHUNKS, 15, 2)), dma((CHUNKS, GROUP, 2)), dma((NQ,)), dma((NX,)),
            dma((4,)), dma((4,)), dma((3,)), dma((3,)), dma((15,)), dma((GROUP,)),
            dma((4, 2)), dma((4, 2)), dma((3, 2)), dma((3, 2)), dma((4,)), dma((NX,)), dma((4,)), dma((NQ,)),
        ],
        compiler_params=pltpu.CompilerParams(
            collective_id=0, has_side_effects=True, vmem_limit_bytes=56 * 1024 * 1024
        ),
    )(acts, probes, facts)
    return pos[None], dep.T[None]


def solution(mesh):
    in_specs = (
        P(None, ("tok", "layer"), None),
        P("layer", None, "tok"),
        P("layer", None, "tok"),
        P(("tok", "layer")),
        P(("tok", "layer")),
        P(("tok", "layer")),
    )
    out_specs = (P("layer", None, "tok"), P("layer", None, "tok"))
    return jax.shard_map(local, mesh=mesh, in_specs=in_specs, out_specs=out_specs, check_vma=False)
```

time: 252 us -> 122 us (0.48)
  blocking collectives: 186 us -> 0 us
  Pallas kernels: 0 us -> 113 us
  local copies, waits for them, and re-layouts: 21.7 us -> 3.83 us
  between operations: 15.4 us -> 1.34 us
  matrix products: 12.3 us -> 0 us
  starting transfers between devices: 12 us -> 0 us
    unnamed x1 -> x0, blocking collectives: 117 us -> none
    pallas_call x0 -> x1, Pallas kernels: none -> 113 us  [local(): pl.pallas_call(kernel, out_shape=(jax.ShapeDtypeStruct((TAGS, 160), F32),...]
    all_to_all x1 -> x0, blocking collectives: 69.1 us -> none  [sum_at_owner(): lax.all_to_all(blocks, axis, split_axis=0, concat_axis=0, tiled=True)]
    dot_general x3 -> x0, matrix products: 12.3 us -> none  [the longest x2 7.53 us: contract(): lax.dot_general(left, right, (((1,), (1,)), ((), ())), preferred_element_...]
    all_to_all x1 -> x0, starting transfers between devices: 12 us -> none  [local(): lax.all_to_all(stacked, 'layer', split_axis=0, concat_axis=1, tiled=True)]
    reshape x2 -> x0, local copies, waits for them, and re-layouts: 10.3 us -> none  [the longest x1 7.25 us: local(): owned_rows = arrived.reshape((-1, arrived.shape[3]))]
    unnamed x19 -> x3, local copies, waits for them, and re-layouts: 9.84 us -> 3.82 us
  transfers between devices with their start and end apart: 2 -> 0, of which waited for: 0 -> 0; matrix products, arithmetic and copies ran while one was open for 4% -> 0% of each run, Pallas kernels for 0% -> 0%
where the time goes in v1:
time: 122 us
  Pallas kernels  113 us (93%)
  local copies, waits for them, and re-layouts  3.83 us (3%)
  other arithmetic  3.31 us (3%)
  between operations  1.34 us (1%)
    pallas_call x1, Pallas kernels, local(): pl.pallas_call(kernel, out_shape=(jax.ShapeDtypeStruct((TAGS, 160), F32),...  113 us
    unnamed x3, local copies, waits for them, and re-layouts  3.82 us

profile of v1, /device:TPU:1, one launch (start us, length us, event | category | flops | bytes accessed | tf_op | source)
XLA Modules:
  0.0 121.6 jit_solution(4834711200405605713)
XLA Ops:
  1.3 0.7 convert_element_type.16
  2.0 0.7 convert_element_type.17
  2.7 0.6 select_maximum_fusion.meta_ref
  3.3 0.9 copy.8
  4.1 1.4 %fusion.2.w_ref = bf16[176,256]{1,0:T(8,128)(2,1)} fusion(bf16[128,160]{1,0:T(8,128)(2,1)S(1)} %bitcast.17, bf16[48,160]{1,0:T(8,128)(2,1)} %bitcast.20), kind=kLoop, calls=%fused_computation.3 | loop fusion | flops 315392 | bytes 146432 | tf_op jit(solution)/shard_map/concatenate | solution.py:292
  5.5 113.1 %shard_map.77 = (f32[48,160]{1,0:T(8,128)}, f32[160,128]{1,0:T(8,128)}) custom-call(bf16[448,5120]{1,0:T(8,128)(2,1)} %bitcast.16, bf16[176,256]{1,0:T(8,128)(2,1)} %fusion.2.w_ref, f32[8,128]{1,0:T(8,128)} %select_maximum_fusion.meta_ref), custom_call_target="tpu_custom_call" | custom-call | tf_op jit(solution)/shard_map/pallas_call | solution.py:299
  118.6 1.4 %copy.12 = f32[1,48,160]{2,1,0:T(8,128)} copy(f32[1,48,160]{2,1,0:T(8,128)} %bitcast.19) | data formatting | bytes 61440
  120.1 1.5 %copy.13 = f32[1,128,160]{1,2,0:T(8,128)} copy(f32[1,128,160]{1,2,0:T(8,128)} %bitcast.18) | data formatting | bytes 163840
  (2 shorter events, 0.0 us)

commit v2 on v1

v2 whole, which is shorter than its diff:
```python
import jax
import jax.numpy as jnp
from jax import lax
from jax.experimental import pallas as pl
from jax.experimental.pallas import tpu as pltpu
from jax.sharding import PartitionSpec as P

MESH = pl.DeviceIdType.MESH
F32, BF16 = jnp.float32, jnp.bfloat16

D, TAGS, RANK, SLOTS = 5120, 48, 128, 28
K = TAGS + RANK
PAD = 32
NX, NY, NQ, NR = 4, 8, 4, 4
GROUP = NX * NR
CHUNKS, WIDE = 4, D // 4
OWN = D // NY
SUBS = ((0, 48), (48, 48), (96, 48), (144, 32))
PARTS = ((0, 24), (24, 4))
PARTNERS = tuple(
    (oc, db, dx) for oc in (0, 1) for db in (0, 1) for dx in (1, 3, 2, 0) if (oc, db, dx) != (0, 0, 0)
)


def wrap(v, n):
    return lax.rem(v + n, n)


def at_z(y, x, z, c):
    return {"tok": y * NX + x, "layer": 2 * z + c}


def pair_of(z, c):
    shifted = wrap(z - c, 8)
    return lax.div(shifted, 2), lax.rem(shifted, 2)


def in_pair(q, b, c):
    return lax.rem(2 * q + b + c, 8)


def send(src, dst, ssem, rsem, device):
    return pltpu.make_async_remote_copy(
        src_ref=src, dst_ref=dst, send_sem=ssem, recv_sem=rsem, device_id=device, device_id_type=MESH
    )


def kernel(
    x_hbm, wp_ref, wd_ref, tags_ref, depths_ref, counts_ref, pos_out, dep_out,
    xin, outbox, rows, wide, wwin, wxp, wxd, wf, meta_own, meta_in, acc, g_ref,
    right_out, right_in, left_out, left_in, mine, r2_in, r3_in,
    load_sem, act_s, act_r, wp_s, wp_r, wd_s, wd_r, wr_s, wr_r, wl_s, wl_r, meta_s, meta_r,
    rr_s, rr_r, rl_s, rl_r, r2_s, r2_r, r3_s, r3_r,
):
    tok, lay = lax.axis_index("tok"), lax.axis_index("layer")
    y, x, z, c = lax.div(tok, NX), lax.rem(tok, NX), lax.div(lay, 2), lax.rem(lay, 2)
    q, b = pair_of(z, c)
    me = x * NR + 2 * b + c
    zi, zb = lax.div(z, 2), lax.rem(z, 2)
    up, down = at_z(wrap(y + 1, NY), x, z, c), at_z(wrap(y - 1, NY), x, z, c)

    def target(i):
        oc, db, dx = PARTNERS[i]
        tc = lax.rem(c + oc, 2)
        tq, tb = pair_of(z, tc)
        px, pb = wrap(x + dx, NX), lax.rem(tb + db, 2)
        return px * NR + 2 * pb + tc, x * NR + 2 * tb + c, at_z(y, px, in_pair(tq, pb, tc), tc)

    def source(i):
        oc, db, dx = PARTNERS[i]
        px, pb, pc = wrap(x + dx, NX), lax.rem(b + db, 2), lax.rem(c + oc, 2)
        return px * NR + 2 * pb + pc, at_z(y, px, in_pair(q, pb, c), pc)

    loads = [
        pltpu.make_async_copy(x_hbm.at[:, pl.ds(k * WIDE, WIDE)], xin.at[k], load_sem.at[k])
        for k in range(CHUNKS)
    ]
    for copy in loads:
        copy.start()
    rows[:, 16:PAD, :] = jnp.zeros((GROUP, PAD - 16, D), BF16)

    barrier = pltpu.get_barrier_semaphore()

    def greet(device):
        pl.semaphore_signal(barrier, inc=1, device_id=device, device_id_type=MESH)

    def owner_z(sq):
        return in_pair(sq, zb, c)

    def home_z(sx):
        return 2 * sx + b

    for i in range(len(PARTNERS)):
        greet(source(i)[1])
    greet(up)
    greet(down)
    expected = len(PARTNERS) + 2
    for n in range(4):
        w_remote = jnp.logical_or(n != x, home_z(x) != z)
        r_remote = owner_z(n) != z
        expected = expected + jnp.logical_or(zi != x, r_remote).astype(jnp.int32)
        expected = expected + (home_z(n) != z).astype(jnp.int32)

        @pl.when(w_remote)
        def _():
            greet(at_z(y, n, home_z(x), c))

        @pl.when(r_remote)
        def _():
            greet(at_z(y, x, owner_z(n), c))

    wide[...] = jnp.zeros_like(wide)
    wide[:, 0:160] = wp_ref[...].astype(F32)
    wwin[...] = pltpu.roll(wide[...], 32 * x, 1).astype(BF16)
    for tc in range(2):
        meta_own[tc] = jnp.zeros((8, 128), F32)
        meta_own[tc, 0:1, 0:SLOTS] = tags_ref[...].astype(F32)
        meta_own[tc, 1:2, 0:SLOTS] = depths_ref[...].astype(F32)
        count = counts_ref[...]
        lane = lax.broadcasted_iota(jnp.int32, (1, SLOTS), 1)
        meta_own[tc, 2:3, 0:SLOTS] = jnp.where(lane < count, 1.0 / count.astype(F32), 0.0)
        meta_own[tc] = pltpu.roll(meta_own[tc], 32 * (2 * pair_of(z, tc)[1] + c), 1)
    pl.semaphore_wait(barrier, expected)

    def w_send(sq):
        device = at_z(y, zi, owner_z(sq), c)
        return (
            send(wwin, wxp.at[x], wp_s.at[sq], wp_r.at[x], device),
            send(wd_ref, wxd.at[x], wd_s.at[sq], wd_r.at[x], device),
        )

    def w_goes(sq):
        return jnp.logical_or(zi != x, owner_z(sq) != z)

    for sq in range(NQ):
        @pl.when(w_goes(sq))
        def _():
            for copy in w_send(sq):
                copy.start()

    @pl.when(jnp.logical_and(home_z(x) == z, zi == x))
    def _():
        wxp[x] = wwin[...]
        wxd[x] = wd_ref[...]

    def meta_send(i):
        _, slot, device = target(i)
        mine_for = meta_own.at[lax.rem(c + PARTNERS[i][0], 2)]
        return send(mine_for, meta_in.at[slot], meta_s.at[i], meta_r.at[slot], device)

    for i in range(len(PARTNERS)):
        meta_send(i).start()
    meta_in[me] = meta_own[c]

    ri = lax.broadcasted_iota(jnp.int32, (256, 256), 0)
    ci = lax.broadcasted_iota(jnp.int32, (256, 256), 1)
    turn = jnp.where(ci == lax.rem(ri, 16) * 16 + lax.div(ri, 16), 1.0, 0.0).astype(BF16)

    def act_send(k, i, j):
        layer, slot, device = target(i)
        lo, n = PARTS[j]
        return send(
            outbox.at[k, layer, pl.ds(lo, n)],
            rows.at[slot, pl.ds(lo, n), pl.ds(k * WIDE, WIDE)],
            act_s.at[k, i, j], act_r.at[k, slot, j], device,
        )

    def turn_and_send(k):
        loads[k].wait()

        @pl.loop(0, WIDE // 256)
        def _(n):
            cols = pl.ds(pl.multiple_of(n * 256, 256), 256)
            first = jnp.dot(turn, xin[k, 0:256, cols], preferred_element_type=F32)
            outbox[k, :, 0:16, cols] = first.astype(BF16).reshape(16, 16, 256)
            last = jnp.dot(turn[:, 0:192], xin[k, 256:448, cols], preferred_element_type=F32)
            outbox[k, :, 16:32, cols] = last.astype(BF16).reshape(16, 16, 256)

        for i in range(len(PARTNERS)):
            for j in range(2):
                act_send(k, i, j).start()
        rows[me, :, k * WIDE:(k + 1) * WIDE] = outbox[k, me]

    for k in range(CHUNKS):
        turn_and_send(k)

    for sx in range(NX):
        @pl.when(jnp.logical_or(sx != x, home_z(x) != z))
        def _():
            device = at_z(y, sx, home_z(x), c)
            send(wwin, wxp.at[sx], wp_s.at[0], wp_r.at[sx], device).wait_recv()
            send(wd_ref, wxd.at[sx], wd_s.at[0], wd_r.at[sx], device).wait_recv()
    for t in range(5):
        part = None
        for sx in (t - 1, t):
            if 0 <= sx < NX:
                lo = 128 * (t - sx)
                v = wxp[sx, :, lo:lo + 128].astype(F32)
                part = v if part is None else part + v
        wf[y, 0:TAGS, 128 * t:128 * (t + 1)] = part.astype(BF16)
    wf[y, TAGS:K] = wxd[...].reshape(OWN, RANK).astype(F32).T.astype(BF16)

    def ring(s, way):
        at = wrap(y - s, NY) if way > 0 else wrap(y + s, NY)
        ss, rs = (wr_s, wr_r) if way > 0 else (wl_s, wl_r)
        return send(wf.at[at], wf.at[at], ss.at[s], rs.at[s], up if way > 0 else down)

    for s in range(4):
        for way, steps in ((1, 4), (-1, 3)):
            if s < steps:
                if s > 0:
                    ring(s - 1, way).wait_recv()
                ring(s, way).start()
    ring(3, 1).wait_recv()
    ring(2, -1).wait_recv()

    acc[...] = jnp.zeros_like(acc)

    @pl.loop(0, CHUNKS)
    def _(k):
        for i in range(len(PARTNERS)):
            slot, device = source(i)
            for j, (lo, n) in enumerate(PARTS):
                send(
                    outbox.at[0, slot, pl.ds(lo, n)],
                    rows.at[slot, pl.ds(lo, n), pl.ds(pl.multiple_of(k * WIDE, WIDE), WIDE)],
                    act_s.at[k, i, j], act_r.at[k, slot, j], device,
                ).wait_recv()
        for h in range(2):
            cols = pl.ds(pl.multiple_of(k * WIDE + h * OWN, 128), OWN)
            acc[...] += lax.dot_general(
                wf[2 * k + h], rows[:, :, cols].reshape(GROUP * PAD, OWN),
                (((1,), (1,)), ((), ())), preferred_element_type=F32,
            )

    for i in range(len(PARTNERS)):
        slot, device = source(i)
        send(meta_own.at[0], meta_in.at[slot], meta_s.at[i], meta_r.at[slot], device).wait_recv()
    facts = jnp.concatenate(
        [sum(meta_in[NR * sx + sr] for sr in range(NR)) for sx in range(NX)], axis=1
    )
    tags, depths, scale = facts[0:1], facts[1:2], facts[2:3]
    logits, hidden = acc[0:TAGS], acc[TAGS:K]
    expo = jnp.exp(logits - jnp.max(logits, axis=0, keepdims=True))
    probs = expo / jnp.sum(expo, axis=0, keepdims=True)
    names = lax.broadcasted_iota(jnp.int32, (TAGS, GROUP * PAD), 0).astype(F32)
    onehot = jnp.where(names == tags, 1.0, 0.0)
    g_ref[0:TAGS] = ((probs - onehot) * scale).astype(BF16)
    predicted = jnp.sum(hidden * hidden, axis=0, keepdims=True)
    g_ref[TAGS:K] = (hidden * ((predicted - depths) * scale)).astype(BF16)

    def block(at, sub):
        lo, n = sub
        cols = pl.ds(pl.multiple_of(at * OWN, 128), OWN)
        return jnp.dot(
            g_ref[lo:lo + n], rows[:, :, cols].reshape(GROUP * PAD, OWN), preferred_element_type=F32
        )

    def hop(s, u, way):
        lo, n = SUBS[u]
        out, inn, ss, rs = (right_out, right_in, rr_s, rr_r) if way > 0 else (left_out, left_in, rl_s, rl_r)
        return send(
            out.at[s, pl.ds(lo, n)], inn.at[s, pl.ds(lo, n)], ss.at[s, u], rs.at[s, u],
            up if way > 0 else down,
        )

    for s in range(4):
        for u, (lo, n) in enumerate(SUBS):
            for way, steps in ((1, 4), (-1, 3)):
                if s >= steps:
                    continue
                out, inn = (right_out, right_in) if way > 0 else (left_out, left_in)
                at = wrap(y + 4 - s, NY) if way > 0 else wrap(y - 3 + s, NY)
                value = block(at, (lo, n))
                if s > 0:
                    hop(s - 1, u, way).wait_recv()
                    value = value + inn[s - 1, lo:lo + n].astype(F32)
                out[s, lo:lo + n] = value.astype(BF16)
                hop(s, u, way).start()
    def window(sx):
        return pl.ds(pl.multiple_of(128 * sx, 128), 256)

    def r2(u, dx):
        px, part = wrap(x + dx, NX), pl.ds(*SUBS[u])
        return send(
            mine.at[part, window(px)], r2_in.at[x, part], r2_s.at[u, dx], r2_r.at[u, x], at_z(y, px, z, c)
        )

    def r3(u, sx):
        part = pl.ds(*SUBS[u])
        return send(
            r2_in.at[sx, part], r3_in.at[q, part], r3_s.at[u, sx], r3_r.at[u, q], at_z(y, x, home_z(sx), c)
        )

    def forward(u):
        lo, n = SUBS[u]
        for dx in (0, 1, 3, 2):
            sx = wrap(x + dx, NX)
            if dx:
                send(
                    mine.at[pl.ds(lo, n), pl.ds(0, 256)], r2_in.at[sx, pl.ds(lo, n)],
                    r2_s.at[u, dx], r2_r.at[u, sx], at_z(y, sx, z, c),
                ).wait_recv()

            @pl.when(home_z(sx) != z)
            def _():
                r3(u, sx).start()

            @pl.when(home_z(sx) == z)
            def _():
                r3_in[q, lo:lo + n] = r2_in[sx, lo:lo + n]

    for u, (lo, n) in enumerate(SUBS):
        value = block(y, (lo, n))
        hop(2, u, -1).wait_recv()
        value = value + left_in[2, lo:lo + n].astype(F32)
        hop(3, u, 1).wait_recv()
        mine[lo:lo + n] = (value + right_in[3, lo:lo + n].astype(F32)).astype(BF16)
        for dx in (1, 3, 2):
            r2(u, dx).start()
        r2_in[x, lo:lo + n] = mine[lo:lo + n, window(x)]
        if u:
            forward(u - 1)
    forward(len(SUBS) - 1)
    for u, (lo, n) in enumerate(SUBS):
        total = jnp.zeros((n, 256), F32)
        for sq in range(NQ):
            @pl.when(owner_z(sq) != z)
            def _():
                send(
                    r2_in.at[0, pl.ds(lo, n)], r3_in.at[sq, pl.ds(lo, n)],
                    r3_s.at[u, 0], r3_r.at[u, sq], at_z(y, x, owner_z(sq), c),
                ).wait_recv()
            total = total + r3_in[sq, lo:lo + n].astype(F32)
        total = pltpu.roll(total, lax.rem(256 - 32 * x, 256), 1)
        if u == 0:
            pos_out[...] = total[:, 0:160]
        else:
            acc[lo:lo + n, 0:256] = total
    dep_out[...] = acc[TAGS:K, 0:256].T[0:160]

    for sq in range(NQ):
        @pl.when(w_goes(sq))
        def _():
            for copy in w_send(sq):
                copy.wait_send()
    for i in range(len(PARTNERS)):
        meta_send(i).wait_send()
        for k in range(CHUNKS):
            for j in range(2):
                act_send(k, i, j).wait_send()
    for s in range(4):
        for way, steps in ((1, 4), (-1, 3)):
            if s < steps:
                ring(s, way).wait_send()
                for u in range(len(SUBS)):
                    hop(s, u, way).wait_send()
    for u in range(len(SUBS)):
        for dx in (1, 3, 2):
            r2(u, dx).wait_send()
        for sx in range(NX):
            @pl.when(home_z(sx) != z)
            def _():
                r3(u, sx).wait_send()


def local(activations, pos_weight, depth_weight, tags, depths, counts):
    acts = jnp.transpose(activations, (1, 0, 2)).reshape(SLOTS * 16, D)
    dma, vm = pltpu.SemaphoreType.DMA, pltpu.VMEM
    in_vmem = pl.BlockSpec(memory_space=vm)
    pos, dep = pl.pallas_call(
        kernel,
        out_shape=(jax.ShapeDtypeStruct((TAGS, 160), F32), jax.ShapeDtypeStruct((160, RANK), F32)),
        in_specs=[pl.BlockSpec(memory_space=pl.ANY)] + [in_vmem] * 5,
        out_specs=(in_vmem, in_vmem),
        scratch_shapes=[
            vm((CHUNKS, SLOTS * 16, WIDE), BF16), vm((CHUNKS, 16, PAD, WIDE), BF16), vm((GROUP, PAD, D), BF16),
            vm((TAGS, 256), F32), vm((TAGS, 256), BF16), vm((NX, TAGS, 256), BF16), vm((NX, 160, RANK), BF16),
            vm((NY, K, OWN), BF16),
            vm((2, 8, 128), F32), vm((GROUP, 8, 128), F32), vm((K, GROUP * PAD), F32), vm((K, GROUP * PAD), BF16),
            vm((4, K, OWN), BF16), vm((4, K, OWN), BF16), vm((3, K, OWN), BF16), vm((3, K, OWN), BF16),
            vm((K, OWN), BF16), vm((NX, K, 256), BF16), vm((NQ, K, 256), BF16),
            dma((CHUNKS,)), dma((CHUNKS, 15, 2)), dma((CHUNKS, GROUP, 2)),
            dma((NQ,)), dma((NX,)), dma((NQ,)), dma((NX,)),
            dma((4,)), dma((4,)), dma((3,)), dma((3,)), dma((15,)), dma((GROUP,)),
            dma((4, 4)), dma((4, 4)), dma((3, 4)), dma((3, 4)), dma((4, 4)), dma((4, NX)), dma((4, NX)), dma((4, NQ)),
        ],
        compiler_params=pltpu.CompilerParams(
            collective_id=0, has_side_effects=True, vmem_limit_bytes=61 * 1024 * 1024
        ),
    )(
        acts, pos_weight[0], depth_weight[0].T,
        tags.reshape(1, SLOTS), depths.reshape(1, SLOTS), counts.reshape(1, 1),
    )
    return pos[None], dep.T[None]


def solution(mesh):
    in_specs = (
        P(None, ("tok", "layer"), None),
        P("layer", None, "tok"),
        P("layer", None, "tok"),
        P(("tok", "layer")),
        P(("tok", "layer")),
        P(("tok", "layer")),
    )
    out_specs = (P("layer", None, "tok"), P("layer", None, "tok"))
    return jax.shard_map(local, mesh=mesh, in_specs=in_specs, out_specs=out_specs, check_vma=False)
```

time: 122 us -> 113 us (0.926)
  Pallas kernels: 113 us -> 109 us
  other arithmetic: 3.31 us -> 0 us
    pallas_call x1, Pallas kernels: 113 us -> 109 us  [local(): pl.pallas_call(kernel, out_shape=(jax.ShapeDtypeStruct((TAGS, 160), F32),...]
    concatenate x1 -> x0, other arithmetic: 1.38 us -> none  [local(): jnp.concatenate([pos_weight[0], depth_weight[0]], axis=0)]
    convert_element_type x2 -> x0, other arithmetic: 1.32 us -> none  [local(): wide = lambda v: jnp.pad(v.astype(F32), (0, 128 - SLOTS))]
    unnamed x3 -> x2, local copies, waits for them, and re-layouts: 3.82 us -> 2.95 us
where the time goes in v2:
time: 113 us
  Pallas kernels  109 us (96%)
  local copies, waits for them, and re-layouts  2.95 us (3%)
  between operations  1.29 us (1%)
    pallas_call x1, Pallas kernels, local(): pl.pallas_call(kernel, out_shape=(jax.ShapeDtypeStruct((TAGS, 160), F32),...  109 us
    unnamed x2, local copies, waits for them, and re-layouts  2.95 us

profile of v2, /device:TPU:1, one launch (start us, length us, event | category | flops | bytes accessed | tf_op | source)
XLA Modules:
  0.0 112.9 jit_solution(1034151134184594993)
XLA Ops:
  1.3 108.7 %shard_map.77 = (f32[48,160]{1,0:T(8,128)}, f32[160,128]{1,0:T(8,128)}) custom-call(bf16[448,5120]{1,0:T(8,128)(2,1)} %bitcast.15, bf16[48,160]{1,0:T(8,128)(2,1)} %bitcast.19, bf16[160,128]{1,0:T(8,128)(2,1)} %bitcast.18, s32[1,28]{1,0:T(1,128)} %bitcast.20, s32[1,28]{1,0:T(1,128)} %bitcast.21, s32[1,1]{1,0:T(1,128)} %bitcast.14.counts_ref), custom_call_target="tpu_custom_call" | custom-call | tf_op jit(solution)/shard_map/pallas_call | solution.py:371
  110.0 1.4 %copy.11 = f32[1,48,160]{2,1,0:T(8,128)} copy(f32[1,48,160]{2,1,0:T(8,128)} %bitcast.17) | data formatting | bytes 61440
  111.4 1.5 %copy.12 = f32[1,128,160]{1,2,0:T(8,128)} copy(f32[1,128,160]{1,2,0:T(8,128)} %bitcast.16) | data formatting | bytes 163840

commit v3 on v2

--- a/solution.py
+++ b/solution.py
@@ -14,6 +14,7 @@
 NX, NY, NQ, NR = 4, 8, 4, 4
 GROUP = NX * NR
 CHUNKS, WIDE = 4, D // 4
+AHEAD = 2
 OWN = D // NY
 SUBS = ((0, 48), (48, 48), (96, 48), (144, 32))
 PARTS = ((0, 24), (24, 4))
@@ -120,6 +121,23 @@
         lane = lax.broadcasted_iota(jnp.int32, (1, SLOTS), 1)
         meta_own[tc, 2:3, 0:SLOTS] = jnp.where(lane < count, 1.0 / count.astype(F32), 0.0)
         meta_own[tc] = pltpu.roll(meta_own[tc], 32 * (2 * pair_of(z, tc)[1] + c), 1)
+    ri = lax.broadcasted_iota(jnp.int32, (256, 256), 0)
+    ci = lax.broadcasted_iota(jnp.int32, (256, 256), 1)
+    turn = jnp.where(ci == lax.rem(ri, 16) * 16 + lax.div(ri, 16), 1.0, 0.0).astype(BF16)
+
+    def relay(k):
+        loads[k].wait()
+
+        @pl.loop(0, WIDE // 256)
+        def _(n):
+            cols = pl.ds(pl.multiple_of(n * 256, 256), 256)
+            head = jnp.dot(turn, xin[k, 0:256, cols], preferred_element_type=F32)
+            outbox[k, :, 0:16, cols] = head.astype(BF16).reshape(16, 16, 256)
+            last = jnp.dot(turn[:, 0:192], xin[k, 256:448, cols], preferred_element_type=F32)
+            outbox[k, :, 16:32, cols] = last.astype(BF16).reshape(16, 16, 256)
+
+    for k in range(AHEAD):
+        relay(k)
     pl.semaphore_wait(barrier, expected)
 
     def w_send(sq):
@@ -151,10 +169,6 @@
     for i in range(len(PARTNERS)):
         meta_send(i).start()
     meta_in[me] = meta_own[c]
-
-    ri = lax.broadcasted_iota(jnp.int32, (256, 256), 0)
-    ci = lax.broadcasted_iota(jnp.int32, (256, 256), 1)
-    turn = jnp.where(ci == lax.rem(ri, 16) * 16 + lax.div(ri, 16), 1.0, 0.0).astype(BF16)
 
     def act_send(k, i, j):
         layer, slot, device = target(i)
@@ -165,24 +179,13 @@
             act_s.at[k, i, j], act_r.at[k, slot, j], device,
         )
 
-    def turn_and_send(k):
-        loads[k].wait()
-
-        @pl.loop(0, WIDE // 256)
-        def _(n):
-            cols = pl.ds(pl.multiple_of(n * 256, 256), 256)
-            first = jnp.dot(turn, xin[k, 0:256, cols], preferred_element_type=F32)
-            outbox[k, :, 0:16, cols] = first.astype(BF16).reshape(16, 16, 256)
-            last = jnp.dot(turn[:, 0:192], xin[k, 256:448, cols], preferred_element_type=F32)
-            outbox[k, :, 16:32, cols] = last.astype(BF16).reshape(16, 16, 256)
-
+    for k in range(CHUNKS):
+        if k >= AHEAD:
+            relay(k)
         for i in range(len(PARTNERS)):
             for j in range(2):
                 act_send(k, i, j).start()
         rows[me, :, k * WIDE:(k + 1) * WIDE] = outbox[k, me]
-
-    for k in range(CHUNKS):
-        turn_and_send(k)
 
     for sx in range(NX):
         @pl.when(jnp.logical_or(sx != x, home_z(x) != z))
@@ -264,15 +267,17 @@
             up if way > 0 else down,
         )
 
+    def first(u, way):
+        return 0 if (u < 2) == (way > 0) else 1
+
     for s in range(4):
         for u, (lo, n) in enumerate(SUBS):
-            for way, steps in ((1, 4), (-1, 3)):
-                if s >= steps:
+            for way in (1, -1):
+                if s < first(u, way):
                     continue
                 out, inn = (right_out, right_in) if way > 0 else (left_out, left_in)
-                at = wrap(y + 4 - s, NY) if way > 0 else wrap(y - 3 + s, NY)
-                value = block(at, (lo, n))
-                if s > 0:
+                value = block(wrap(y + way * (4 - s), NY), (lo, n))
+                if s > first(u, way):
                     hop(s - 1, u, way).wait_recv()
                     value = value + inn[s - 1, lo:lo + n].astype(F32)
                 out[s, lo:lo + n] = value.astype(BF16)
@@ -312,8 +317,8 @@
 
     for u, (lo, n) in enumerate(SUBS):
         value = block(y, (lo, n))
-        hop(2, u, -1).wait_recv()
-        value = value + left_in[2, lo:lo + n].astype(F32)
+        hop(3, u, -1).wait_recv()
+        value = value + left_in[3, lo:lo + n].astype(F32)
         hop(3, u, 1).wait_recv()
         mine[lo:lo + n] = (value + right_in[3, lo:lo + n].astype(F32)).astype(BF16)
         for dx in (1, 3, 2):
@@ -353,7 +358,8 @@
         for way, steps in ((1, 4), (-1, 3)):
             if s < steps:
                 ring(s, way).wait_send()
-                for u in range(len(SUBS)):
+            for u in range(len(SUBS)):
+                if s >= first(u, way):
                     hop(s, u, way).wait_send()
     for u in range(len(SUBS)):
         for dx in (1, 3, 2):
@@ -378,12 +384,12 @@
             vm((TAGS, 256), F32), vm((TAGS, 256), BF16), vm((NX, TAGS, 256), BF16), vm((NX, 160, RANK), BF16),
             vm((NY, K, OWN), BF16),
             vm((2, 8, 128), F32), vm((GROUP, 8, 128), F32), vm((K, GROUP * PAD), F32), vm((K, GROUP * PAD), BF16),
-            vm((4, K, OWN), BF16), vm((4, K, OWN), BF16), vm((3, K, OWN), BF16), vm((3, K, OWN), BF16),
+            vm((4, K, OWN), BF16), vm((4, K, OWN), BF16), vm((4, K, OWN), BF16), vm((4, K, OWN), BF16),
             vm((K, OWN), BF16), vm((NX, K, 256), BF16), vm((NQ, K, 256), BF16),
             dma((CHUNKS,)), dma((CHUNKS, 15, 2)), dma((CHUNKS, GROUP, 2)),
             dma((NQ,)), dma((NX,)), dma((NQ,)), dma((NX,)),
             dma((4,)), dma((4,)), dma((3,)), dma((3,)), dma((15,)), dma((GROUP,)),
-            dma((4, 4)), dma((4, 4)), dma((3, 4)), dma((3, 4)), dma((4, 4)), dma((4, NX)), dma((4, NX)), dma((4, NQ)),
+            dma((4, 4)), dma((4, 4)), dma((4, 4)), dma((4, 4)), dma((4, 4)), dma((4, NX)), dma((4, NX)), dma((4, NQ)),
         ],
         compiler_params=pltpu.CompilerParams(
             collective_id=0, has_side_effects=True, vmem_limit_bytes=61 * 1024 * 1024

time: 113 us -> 111 us (0.982); the launches traced: 113 us -> 110 us
  Pallas kernels: 109 us -> 106 us
    pallas_call x1, Pallas kernels: 109 us -> 106 us  [local(): pl.pallas_call(kernel, out_shape=(jax.ShapeDtypeStruct((TAGS, 160), F32),...]
where the time goes in v3:
time: 111 us; the launch traced here: 110 us
  Pallas kernels  106 us (95%)
  local copies, waits for them, and re-layouts  2.95 us (3%)
  between operations  1.29 us (1%)
    pallas_call x1, Pallas kernels, local(): pl.pallas_call(kernel, out_shape=(jax.ShapeDtypeStruct((TAGS, 160), F32),...  106 us
    unnamed x2, local copies, waits for them, and re-layouts  2.95 us

profile of v3, /device:TPU:1, one launch (start us, length us, event | category | flops | bytes accessed | tf_op | source)
XLA Modules:
  0.0 109.7 jit_solution(13764271707139807388)
XLA Ops:
  1.3 105.5 %shard_map.77 = (f32[48,160]{1,0:T(8,128)}, f32[160,128]{1,0:T(8,128)}) custom-call(bf16[448,5120]{1,0:T(8,128)(2,1)} %bitcast.15, bf16[48,160]{1,0:T(8,128)(2,1)} %bitcast.19, bf16[160,128]{1,0:T(8,128)(2,1)} %bitcast.18, s32[1,28]{1,0:T(1,128)} %bitcast.20, s32[1,28]{1,0:T(1,128)} %bitcast.21, s32[1,1]{1,0:T(1,128)} %bitcast.14.counts_ref), custom_call_target="tpu_custom_call" | custom-call | tf_op jit(solution)/shard_map/pallas_call | solution.py:377
  106.8 1.4 %copy.11 = f32[1,48,160]{2,1,0:T(8,128)} copy(f32[1,48,160]{2,1,0:T(8,128)} %bitcast.17) | data formatting | bytes 61440
  108.2 1.5 %copy.12 = f32[1,128,160]{1,2,0:T(8,128)} copy(f32[1,128,160]{1,2,0:T(8,128)} %bitcast.16) | data formatting | bytes 163840

commit v4 on v3

--- a/solution.py
+++ b/solution.py
@@ -19,7 +19,7 @@
 SUBS = ((0, 48), (48, 48), (96, 48), (144, 32))
 PARTS = ((0, 24), (24, 4))
 PARTNERS = tuple(
-    (oc, db, dx) for oc in (0, 1) for db in (0, 1) for dx in (1, 3, 2, 0) if (oc, db, dx) != (0, 0, 0)
+    (oc, db, dx) for db in (1, 0) for oc in (0, 1) for dx in (2, 1, 3, 0) if (oc, db, dx) != (0, 0, 0)
 )
 
 

time: 111 us -> 111 us (level)
  no operation moved by 1% of the time
where the time goes in v4:
time: 111 us; the launch traced here: 110 us
  Pallas kernels  106 us (95%)
  local copies, waits for them, and re-layouts  2.95 us (3%)
  between operations  1.29 us (1%)
    pallas_call x1, Pallas kernels, local(): pl.pallas_call(kernel, out_shape=(jax.ShapeDtypeStruct((TAGS, 160), F32),...  106 us
    unnamed x2, local copies, waits for them, and re-layouts  2.95 us

profile of v4, /device:TPU:1, one launch (start us, length us, event | category | flops | bytes accessed | tf_op | source)
XLA Modules:
  0.0 110.5 jit_solution(17643163281773614581)
XLA Ops:
  1.3 106.2 %shard_map.77 = (f32[48,160]{1,0:T(8,128)}, f32[160,128]{1,0:T(8,128)}) custom-call(bf16[448,5120]{1,0:T(8,128)(2,1)} %bitcast.15, bf16[48,160]{1,0:T(8,128)(2,1)} %bitcast.19, bf16[160,128]{1,0:T(8,128)(2,1)} %bitcast.18, s32[1,28]{1,0:T(1,128)} %bitcast.20, s32[1,28]{1,0:T(1,128)} %bitcast.21, s32[1,1]{1,0:T(1,128)} %bitcast.14.counts_ref), custom_call_target="tpu_custom_call" | custom-call | tf_op jit(solution)/shard_map/pallas_call | solution.py:377
  107.5 1.4 %copy.11 = f32[1,48,160]{2,1,0:T(8,128)} copy(f32[1,48,160]{2,1,0:T(8,128)} %bitcast.17) | data formatting | bytes 61440
  108.9 1.5 %copy.12 = f32[1,128,160]{1,2,0:T(8,128)} copy(f32[1,128,160]{1,2,0:T(8,128)} %bitcast.16) | data formatting | bytes 163840
